TPU v7x, 256 devices: a whole 4x4x8 slice. The times are simulated.
256 devices in a mesh: tm: 8 (over z), row: 8 (over x, core), obs: 4 (over y).
Axes of the slice: x: 4, y: 4, z: 8, core: 2. Of those that a mesh axis runs over, the one named last changes fastest.
Arguments:
- dyn_pattern: int32 [16, 8, 3], P('tm'), may hold values from 0 to 7
- dyn_values: float32 [16, 1024, 384], P('tm', ('row', 'obs')), may hold values from -0.3125 to 0.3125
- offsets: float32 [16, 1024], P('tm', ('row', 'obs')), may hold values from -6 to 6
- covariance: float32 [16, 1024, 1024], P('tm', ('row', 'obs')), may hold values from -1 to 14, as said below
- obs_block: int32 [16, 128], P('tm'), may hold values from 0 to 7
- obs_matrix: float32 [16, 128, 256], P('tm', 'obs'), may hold values from -0.375 to 0.375
- obs_data: float32 [16, 128], P('tm', 'obs'), may hold values from -6 to 6
Outputs:
- scan_dynamics: float32 [8, 1024, 1024], P('tm', ('row', 'obs'))
- scan_offset: float32 [8, 1024], P('tm', ('row', 'obs'))
- scan_covariance: float32 [8, 1024, 1024], P('tm', ('row', 'obs'))
- scan_factor: float32 [8, 1024, 512], P('tm', ('row', 'obs'))
- scan_information: float32 [8, 1024], P('tm', ('row', 'obs'))
Inputs may be any that keep to these rules, and one draw needn't show every extreme that they name: `dyn_pattern`: each entry names a block column. `obs_block`: each entry names a state block. Each covariance is symmetric and positive definite.
All inputs are finite; a program needn't handle non-finite values.
Results may differ from a plain program's by a relative error of at most 0.00019.
Values sent between devices are 32-bit elements; how exact they have to be, the bound alone decides.
A program may use at most 128 MiB of HBM per device.

v0:
```python
import jax
import jax.numpy as jnp
from jax import lax
from jax.sharding import PartitionSpec as P

largest_value = lax.Precision.HIGHEST


def shifted(block, axis, distance):
    devices = range(lax.axis_size(axis))
    route = [(i - distance, i) for i in devices if i - distance in devices]
    return lax.ppermute(block, axis, route)


def product(left, right):
    return jnp.dot(left, right, precision=largest_value, preferred_element_type=jnp.float32)


def lower_solve(lower, rhs):
    return lax.linalg.triangular_solve(lower, rhs, left_side=True, lower=True)


def assemble_dynamics(pattern, values):
    number_of_blocks = pattern.shape[0]
    per_row = pattern.shape[1]
    states = values.shape[0]
    block_extent = states // number_of_blocks
    indicator_matrix = (
        pattern[:, :, None] == jnp.arange(number_of_blocks, dtype=jnp.int32)[None, None, :]
    ).astype(jnp.float32)
    blocks = values.reshape(number_of_blocks, block_extent, per_row, block_extent)
    return jnp.einsum("ckd,cikj->cidj", indicator_matrix, blocks, precision=largest_value).reshape(
        states, states
    )


def assemble_factor(indices, matrix, number_of_blocks):
    item_count = matrix.shape[0]
    block_extent = matrix.shape[1] // 2
    reach = (indices[:, None] + jnp.arange(2, dtype=jnp.int32)[None, :]) % number_of_blocks
    indicator_matrix = (
        reach[:, :, None] == jnp.arange(number_of_blocks, dtype=jnp.int32)[None, None, :]
    ).astype(jnp.float32)
    piece_list = matrix.reshape(item_count, 2, block_extent)
    return jnp.einsum(
        "onr,onz->rzo", indicator_matrix, piece_list, precision=largest_value
    ).reshape(number_of_blocks * block_extent, item_count)


def combine(
    prior_dyn,
    prior_offsets,
    prior_cov,
    prior_factor,
    prior_zeta,
    own_dyn,
    own_offsets,
    own_cov,
    own_factor,
    own_zeta,
    row_start,
):
    panel_rows = prior_cov.shape[0]
    rank_width = own_factor.shape[1]
    own_pan = lax.dynamic_slice_in_dim(own_dyn, row_start, panel_rows, 0)
    gain_pan = product(prior_cov, own_factor)
    gain_rows = lax.all_gather(gain_pan, ("row", "obs"), axis=0, tiled=True)
    identity = jnp.eye(rank_width, dtype=jnp.float32)
    factor_pan = lax.dynamic_slice_in_dim(own_factor, row_start, panel_rows, 0)
    system = identity + lax.psum(product(factor_pan.T, gain_pan), ("row", "obs"))
    lower = jnp.linalg.cholesky(system)
    carried = product(own_dyn, gain_rows)
    observed = product(prior_dyn.T, own_factor)
    upper_part = lower_solve(lower, observed.T)
    weights = lower_solve(lower, carried.T).T
    weight_pan = lax.dynamic_slice_in_dim(weights, row_start, panel_rows, 0)
    spread_pan = product(prior_cov, own_dyn.T)
    moved = product(own_pan, lax.all_gather(spread_pan, ("row", "obs"), axis=0, tiled=True))
    new_dyn = product(own_pan, prior_dyn) - product(weight_pan, upper_part)
    new_cov = moved - product(weight_pan, weights.T) + own_cov
    residual = own_zeta - product(own_factor.T, prior_offsets)
    solved = lower_solve(lower, residual[:, None])[:, 0]
    new_offsets = product(own_pan, prior_offsets) + product(weight_pan, solved) + own_offsets
    upper_pan = lax.dynamic_slice_in_dim(upper_part, row_start, panel_rows, 1).T
    new_factor = jnp.concatenate([upper_pan, prior_factor], axis=1)
    new_zeta = jnp.concatenate([solved, prior_zeta])
    return (new_dyn, new_offsets, new_cov, new_factor, new_zeta)


def per_device(dyn_pattern, dyn_values, offsets, covariance, obs_block, obs_matrix, obs_data):
    panel_rows = covariance.shape[1]
    row_start = lax.axis_index(("row", "obs")) * panel_rows
    number_of_blocks = dyn_pattern.shape[1]
    obs_rows, obs_values = (
        lax.all_gather(obs_matrix, "obs", axis=1, tiled=True),
        lax.all_gather(obs_data, "obs", axis=1, tiled=True),
    )
    row_values, row_offsets = (
        lax.all_gather(dyn_values, ("row", "obs"), axis=1, tiled=True),
        lax.all_gather(offsets, ("row", "obs"), axis=1, tiled=True),
    )
    first_dyn = assemble_dynamics(dyn_pattern[0], row_values[0])
    second_dyn = assemble_dynamics(dyn_pattern[1], row_values[1])
    first_factor = assemble_factor(obs_block[0], obs_rows[0], number_of_blocks)
    second_factor = assemble_factor(obs_block[1], obs_rows[1], number_of_blocks)
    first_pan = lax.dynamic_slice_in_dim(first_factor, row_start, panel_rows, 0)
    dyn_pan, off_pan, cov_pan, fac_pan, zeta_full = combine(
        first_dyn,
        row_offsets[0],
        covariance[0],
        first_pan,
        obs_values[0],
        second_dyn,
        offsets[1],
        covariance[1],
        second_factor,
        obs_values[1],
        row_start,
    )
    later_pan, later_cov, later_off, later_fac, later_zeta = shifted(
        (dyn_pan, cov_pan, off_pan, fac_pan, zeta_full), "tm", -1
    )
    prior_full, later_full, later_factor, prior_offsets = (
        lax.all_gather(dyn_pan, ("row", "obs"), axis=0, tiled=True),
        lax.all_gather(later_pan, ("row", "obs"), axis=0, tiled=True),
        lax.all_gather(later_fac, ("row", "obs"), axis=0, tiled=True),
        lax.all_gather(off_pan, ("row", "obs"), axis=0, tiled=True),
    )
    top_dyn, top_off, top_cov, top_fac, top_zeta = combine(
        prior_full,
        prior_offsets,
        cov_pan,
        fac_pan,
        zeta_full,
        later_full,
        later_off,
        later_cov,
        later_factor,
        later_zeta,
        row_start,
    )
    even_turn = lax.axis_index("tm") % 2 == 0
    padded_fac = jnp.concatenate([fac_pan, jnp.zeros_like(fac_pan)], axis=1)
    padded_zeta = jnp.concatenate([zeta_full, jnp.zeros_like(zeta_full)])
    out_dyn = jnp.where(even_turn, top_dyn, dyn_pan)
    out_off = jnp.where(even_turn, top_off, off_pan)
    out_cov = jnp.where(even_turn, top_cov, cov_pan)
    out_fac = jnp.where(even_turn, top_fac, padded_fac)
    out_zeta = jnp.where(even_turn, top_zeta, padded_zeta)
    output_information = product(out_fac, out_zeta)
    return (out_dyn[None], out_off[None], out_cov[None], out_fac[None], output_information[None])


def solution(mesh):
    placed = (
        P("tm", None, None),
        P("tm", ("row", "obs"), None),
        P("tm", ("row", "obs")),
        P("tm", ("row", "obs"), None),
        P("tm", None),
        P("tm", "obs", None),
        P("tm", "obs"),
    )
    return jax.shard_map(
        per_device,
        mesh=mesh,
        in_specs=placed,
        out_specs=(
            P("tm", ("row", "obs"), None),
            P("tm", ("row", "obs")),
            P("tm", ("row", "obs"), None),
            P("tm", ("row", "obs"), None),
            P("tm", ("row", "obs")),
        ),
        check_vma=False,
    )
```

profile of v0, /device:TPU:1, one launch (start us, length us, event | category | flops | bytes accessed | tf_op | source)
XLA Modules:
  0.0 616.6 jit_solution(8064863237237655006)
XLA Ops:
  8.0 11.5 %all_gather.37 = f32[2,128,256]{2,1,0:T(8,128)S(1)} all-gather(f32[2,32,256]{2,1,0:T(8,128)} %param.16), channel_id=1, replica_groups=mesh['tm'=8,'row'=8,'obs'=4] {'obs'}, dimensions={1}, use_global_device_ids=true | all-gather | bytes 327680 | tf_op jit(solution)/shard_map/all_gather | solution.py:95
  24.0 40.9 %all-gather.10.cloned.1.call-done = f32[2,1024,384]{2,1,0:T(8,128)} async-done(((f32[2,32,384]{2,1,0:T(8,128)}), f32[2,1024,384]{2,1,0:T(8,128)}) %all-gather.10.cloned.1.call-update) | async-done | bytes 3145744 | tf_op jit(solution)/shard_map/all_gather | solution.py:99
  64.9 3.2 fusion.135
  68.2 3.6 reshape.312
  71.8 4.3 fusion.104
  78.1 4.9 convolution_bitcast_fusion.1
  84.7 89.2 %all-reduce.5.cloned.1.call-done = f32[128,128]{1,0:T(8,128)} async-done(((f32[128,128]{1,0:T(8,128)}), f32[128,128]{1,0:T(8,128)}) %all-reduce.5.cloned.1.call-update) | async-done | bytes 65552 | tf_op jit(solution)/shard_map/psum | solution.py:70
  175.6 11.7 %cholesky.60 = f32[128,128]{1,0:T(8,128)S(1)} custom-call(f32[128,128]{1,0:T(8,128)S(1)} %fusion.77), custom_call_target="Cholesky" | custom-call | tf_op jit(solution)/shard_map/jit(cholesky)/cholesky | solution.py:71
  188.7 9.8 %custom-call.31 = f32[1,128,128]{1,2,0:T(8,128)S(1)} custom-call(f32[1,128,128]{2,1,0:T(8,128)S(1)} %fusion.55), custom_call_target="InvertDiagBlocksLowerTriangular" | custom-call | tf_op jit(solution)/shard_map/triangular_solve/custom-call.4 | solution.py:20
  200.7 4.3 fusion.107
  207.1 3.0 fusion
  212.1 3.8 collective-permute-done.1
  216.6 42.6 %all_gather.38 = f32[1024,128]{1,0:T(8,128)S(1)} all-gather(f32[32,128]{1,0:T(8,128)S(1)} %bitcast.273), channel_id=1, replica_groups=mesh['tm'=8,'row'=8,'obs'=4] {'row','obs'}, dimensions={0}, use_global_device_ids=true | all-gather | bytes 540672 | tf_op jit(solution)/shard_map/all_gather | solution.py:67
  259.2 3.4 copy.79
  262.6 4.8 fusion.133
  273.0 4.4 collective-permute-done
  278.9 4.8 fusion.52
  288.9 40.2 %all-gather = f32[32,32,2]{1,2,0:T(2,128)S(1)} all-gather(f32[1,32,2]{1,2,0:T(2,128)S(1)} %bitcast.282), channel_id=1, replica_groups=mesh['tm'=8,'row'=8,'obs'=4] {'row','obs'}, dimensions={0}, use_global_device_ids=true | all-gather | bytes 8448 | tf_op jit(solution)/shard_map/all_gather | solution.py:100
  329.1 5.2 all-gather.1
  335.7 6.7 %fusion.141 = f32[32,1024]{1,0:T(8,128)} fusion(f32[32,1024]{1,0:T(8,128)S(1)} %fusion.12, f32[1024,1024]{1,0:T(8,128)} %all-gather.12.cloned.1.call-done), kind=kOutput, calls=%fused_computation.205 | convolution fusion | flops 402653184 | bytes 4456448 | tf_op jit(solution)/shard_map/dot_general | solution.py:16
  348.2 63.2 %all-reduce.1 = f32[1024]{0:T(1024)S(1)} all-reduce(f32[1024]{0:T(1024)S(1)} %dynamic-update-slice.17), channel_id=1, replica_groups=mesh['tm'=8,'row'=8,'obs'=4] {'row','obs'}, use_global_device_ids=true, to_apply=%add.1 | all-reduce | flops 1024 | bytes 8192
  413.4 6.0 fusion.140
  419.4 80.5 %all-reduce.7.cloned.1.call-done = f32[256,256]{0,1:T(8,128)} async-done(((f32[256,256]{0,1:T(8,128)}), f32[256,256]{0,1:T(8,128)}) %all-reduce.7.cloned.1.call-update) | async-done | bytes 262160 | tf_op jit(solution)/shard_map/psum | solution.py:70
  502.0 11.7 %cholesky.115 = f32[128,128]{1,0:T(8,128)S(1)} custom-call(f32[128,128]{1,0:T(8,128)S(1)} %cholesky.141), custom_call_target="Cholesky" | custom-call | tf_op jit(solution)/shard_map/jit(cholesky)/cholesky | solution.py:71
  513.8 9.8 %custom-call.26 = f32[1,128,128]{1,2,0:T(8,128)S(1)} custom-call(f32[1,128,128]{2,1,0:T(8,128)S(1)} %get-tuple-element.62), custom_call_target="InvertDiagBlocksLowerTriangular" | custom-call | tf_op jit(solution)/shard_map/jit(cholesky)/cholesky | solution.py:71
  524.1 11.7 %cholesky.128 = f32[128,128]{1,0:T(8,128)S(1)} custom-call(f32[128,128]{1,0:T(8,128)S(1)} %convolution_subtract_fusion.3), custom_call_target="Cholesky" | custom-call | tf_op jit(solution)/shard_map/jit(cholesky)/cholesky | solution.py:71
  538.5 4.0 while.5
  542.5 19.8 %custom-call.33 = f32[2,128,128]{1,2,0:T(8,128)S(1)} custom-call(f32[2,128,128]{2,1,0:T(8,128)S(1)} %get-tuple-element.29), custom_call_target="InvertDiagBlocksLowerTriangular" | custom-call | tf_op jit(solution)/shard_map/triangular_solve/custom-call.5 | solution.py:20
  566.5 9.2 %fusion.139 = f32[256,1024]{1,0:T(8,128)S(1)} fusion(f32[1024,256]{1,0:T(8,128)} %all-gather.20.cloned.1.call-done, f32[1024,1024]{1,0:T(8,128)} %all-gather.12.cloned.1.call-done), kind=kOutput, calls=%fused_computation.203 | convolution fusion | flops 3221225472 | bytes 6291456 | tf_op jit(solution)/shard_map/dot_general | solution.py:16
  579.2 4.1 fusion.14
  585.1 19.4 %all-gather.22.cloned.1.call-done = f32[1024,1024]{1,0:T(8,128)} async-done(((f32[32,1024]{1,0:T(8,128)}), f32[1024,1024]{1,0:T(8,128)}) %all-gather.22.cloned.1.call-update) | async-done | bytes 4194320 | tf_op jit(solution)/shard_map/all_gather | solution.py:78
  604.5 5.4 fusion.11
  (159 shorter events, 56.9 us)
Async XLA Ops:
  7.2 16.8 %copy-start.15 = (s32[2,8,3]{1,0,2:T(2,128)S(1)}, s32[2,8,3]{1,0,2:T(2,128)}, u32[]{:S(2)}) copy-start(s32[2,8,3]{1,0,2:T(2,128)} %param.11) | copy-start | bytes 580
  7.2 57.8 %all-gather.10.cloned.1.call-start = ((), (), s32[]{:S(2)}) async-start(), calls=%async_computation | async-start | bytes 3244032 | tf_op jit(solution)/shard_map/all_gather | solution.py:99
  7.9 165.9 %all-reduce.5.cloned.1.call-start = ((), (), s32[]{:S(2)}) async-start(), calls=%async_computation.1 | async-start | bytes 131072 | tf_op jit(solution)/shard_map/psum | solution.py:70
  23.9 255.0 %all-gather.18.cloned.1.call-start = ((), (), s32[]{:S(2)}) async-start(), calls=%async_computation.5 | async-start | bytes 4325376 | tf_op jit(solution)/shard_map/all_gather | solution.py:78
  68.2 9.9 %copy-start.10 = (f32[2,32,1024]{2,1,0:T(8,128)S(1)}, f32[2,32,1024]{2,1,0:T(8,128)}, u32[]{:S(2)}) copy-start(f32[2,32,1024]{2,1,0:T(8,128)} %param.14) | copy-start | bytes 786436
  76.1 2.0 copy-start
  83.0 201.2 %all-gather.16.cloned.1.call-start = ((), (), s32[]{:S(2)}) async-start(), calls=%async_computation.4 | async-start | bytes 1081344 | tf_op jit(solution)/shard_map/all_gather | solution.py:126
  84.6 120.4 %copy-start.9 = (f32[8,128,128]{2,1,0:T(8,128)}, f32[8,128,128]{2,1,0:T(8,128)S(1)}, u32[]{:S(2)}) copy-start(f32[8,128,128]{2,1,0:T(8,128)S(1)} %copy.56) | copy-start | bytes 1572868
  205.0 2.0 copy-start.2
  210.9 5.0 collective-permute-start.1
  215.9 0.6 copy-start.13
  216.5 119.2 %all-gather.12.cloned.1.call-start = ((), (), s32[]{:S(2)}) async-start(), calls=%async_computation.2 | async-start | bytes 4325376 | tf_op jit(solution)/shard_map/all_gather | solution.py:125
  259.2 3.5 copy-start.1
  262.6 5.9 copy-start.6
  262.6 5.9 copy-start.3
  271.5 6.6 %copy-start.7 = (f32[32,1024]{1,0:T(8,128)}, f32[32,1024]{1,0:T(8,128)S(1)}, u32[]{:S(2)}) copy-start(f32[32,1024]{1,0:T(8,128)S(1)} %fusion.6) | copy-start | bytes 393220
  271.5 17.3 %copy-start.14 = (f32[2,32]{1,0:T(2,128)S(1)}, f32[2,32]{1,0:T(2,128)}, u32[]{:S(2)}) copy-start(f32[2,32]{1,0:T(2,128)} %param.13) | copy-start | bytes 772
  271.5 57.6 %copy-start.16 = (f32[2,32]{1,0:T(2,128)S(1)}, f32[2,32]{1,0:T(2,128)}, u32[]{:S(2)}) copy-start(f32[2,32]{1,0:T(2,128)} %param.17) | copy-start | bytes 772
  271.5 5.8 collective-permute-start
  277.4 0.7 copy-start.12
  278.1 135.3 %all-gather.14.cloned.1.call-start = ((), (), s32[]{:S(2)}) async-start(), calls=%async_computation.3 | async-start | bytes 4325376 | tf_op jit(solution)/shard_map/all_gather | solution.py:124
  278.6 221.2 %all-reduce.7.cloned.1.call-start = ((), (), s32[]{:S(2)}) async-start(), calls=%async_computation.6 | async-start | bytes 524288 | tf_op jit(solution)/shard_map/psum | solution.py:70
  283.7 58.8 %copy-start.17 = (u32[256]{0:T(256)S(1)}, u32[256]{0:T(256)}, u32[]{:S(2)}) copy-start(u32[256]{0:T(256)} %constant.217) | copy-start | bytes 3076
  284.2 127.2 %copy-start.5 = (f32[1024,256]{1,0:T(8,128)S(1)}, f32[1024,256]{1,0:T(8,128)}, u32[]{:S(2)}) copy-start(f32[1024,256]{1,0:T(8,128)} %all-gather.16.cloned.1.call-done) | copy-start | bytes 3145732
  286.1 2.0 copy-start.11
  288.1 278.4 %all-gather.20.cloned.1.call-start = ((), (), s32[]{:S(2)}) async-start(), calls=%async_computation.7 | async-start | bytes 1081344 | tf_op jit(solution)/shard_map/all_gather | solution.py:67
  288.8 315.7 %all-gather.22.cloned.1.call-start = ((), (), s32[]{:S(2)}) async-start(), calls=%async_computation.8 | async-start | bytes 4325376 | tf_op jit(solution)/shard_map/all_gather | solution.py:78
  343.9 68.2 %collective-permute-start.2 = (f32[256]{0:T(256)S(1)}, f32[256]{0:T(256)S(1)}, u32[]{:S(2)}, u32[]{:S(2)}) collective-permute-start(f32[256]{0:T(256)S(1)} %pad_maximum_fusion.5), channel_id=1, source_target_pairs={{32,0},{64,32},{96,64},{128,96},{160,128},{192,160},{224,192},{33,... | collective-permute-start | bytes 3080 | tf_op jit(solution)/shard_map/ppermute | solution.py:12
  346.6 236.8 %collective-permute-start.3 = (f32[32]{0:T(128)S(1)}, f32[32]{0:T(128)S(1)}, u32[]{:S(2)}, u32[]{:S(2)}) collective-permute-start(f32[32]{0:T(128)S(1)} %fusion.16), channel_id=1, source_target_pairs={{32,0},{64,32},{96,64},{128,96},{160,128},{192,160},{224,192},{33,... | collective-permute-start | bytes 392 | tf_op jit(solution)/shard_map/ppermute | solution.py:12
  412.1 173.0 %collective-permute-start.4 = (f32[32,1024]{1,0:T(8,128)S(1)}, f32[32,1024]{1,0:T(8,128)S(1)}, u32[]{:S(2)}, u32[]{:S(2)}) collective-permute-start(f32[32,1024]{1,0:T(8,128)S(1)} %fusion.12), channel_id=1, source_target_pairs={{32,0},{64,32},{96,64},{128,96},{160,128},{192,160},{224,192},{33,... | collective-permute-start | bytes 393224 | tf_op jit(solution)/shard_map/ppermute | solution.py:12
  575.7 3.5 copy-start.4
  575.7 3.5 copy-start.8
Sparse Core Ops, SparseCore 0:
  10.6 54.3 all-gather.9
  68.8 104.9 all-reduce.4
  177.3 50.7 all-gather.17
  231.4 47.2 all-gather.15
  281.4 50.4 all-gather.11
  335.2 50.5 all-gather.13
  389.4 110.4 all-reduce.6
  503.0 48.6 all-gather.19
  554.3 50.1 all-gather.21
where the time goes:
time: 624 us; the launch traced here: 617 us
  waiting for transfers between devices  240 us (38%)
  blocking collectives  163 us (26%)
  other arithmetic  82 us (13%)
  matrix products  81.8 us (13%)
  local copies, waits for them, and re-layouts  25.7 us (4%)
  between operations  16.7 us (3%)
  starting transfers between devices  7.45 us (1%)
    psum x2, waiting for transfers between devices, combine(): lax.psum(product(factor_pan.T, gain_pan), ('row', 'obs'))  170 us
    dot_general x25, matrix products, product(): jnp.dot(left, right, precision=largest_value, preferred_element_type=jnp....  65.3 us
    unnamed x1, blocking collectives  63.2 us
    another operation x10, other arithmetic, combine(): lower = jnp.linalg.cholesky(system)  47 us
    all_gather x1, blocking collectives, combine(): gain_rows = lax.all_gather(gain_pan, ('row', 'obs'), axis=0, tiled=True)  42.6 us
    all_gather x1, waiting for transfers between devices, per_device(): lax.all_gather(dyn_values, ('row', 'obs'), axis=1, tiled=True)  40.9 us
    all_gather x1, blocking collectives, per_device(): lax.all_gather(offsets, ('row', 'obs'), axis=1, tiled=True)  40.2 us
    another operation x8, other arithmetic, lower_solve(): return lax.linalg.triangular_solve(lower, rhs, left_side=True, lower=True)  30.5 us
  transfers between devices with their start and end apart: 14, of which 6 were waited for; matrix products, arithmetic and copies ran while one was open for 29% of the time, Pallas kernels for 0%

commit v1 on v0

--- a/solution.py
+++ b/solution.py
@@ -2,6 +2,7 @@
 import jax.numpy as jnp
 from jax import lax
 from jax.sharding import PartitionSpec as P
+from jax.lax import psum
 
 largest_value = lax.Precision.HIGHEST
 
@@ -67,7 +68,11 @@
     gain_rows = lax.all_gather(gain_pan, ("row", "obs"), axis=0, tiled=True)
     identity = jnp.eye(rank_width, dtype=jnp.float32)
     factor_pan = lax.dynamic_slice_in_dim(own_factor, row_start, panel_rows, 0)
-    system = identity + lax.psum(product(factor_pan.T, gain_pan), ("row", "obs"))
+
+    def limits_produce(own_rows, axis_id, mesh_ax):
+        return psum(psum(own_rows, axis_name=axis_id), axis_name=mesh_ax)
+
+    system = identity + limits_produce(product(factor_pan.T, gain_pan), "obs", "row")
     lower = jnp.linalg.cholesky(system)
     carried = product(own_dyn, gain_rows)
     observed = product(prior_dyn.T, own_factor)

time: 624 us -> 538 us (0.86)
  the two profiles are of different devices: /device:TPU:1 before, /device:TPU:224 now
where the time goes in v1:
time: 538 us; the launch traced here: 530 us
  blocking collectives  168 us (31%)
  waiting for transfers between devices  132 us (25%)
  matrix products  83.9 us (16%)
  other arithmetic  82.1 us (15%)
  local copies, waits for them, and re-layouts  27.2 us (5%)
  starting transfers between devices  18.5 us (3%)
  between operations  18.5 us (3%)
    psum x4, waiting for transfers between devices, limits_produce(): return psum(psum(own_rows, axis_name=axis_id), axis_name=mesh_ax)  119 us
    dot_general x25, matrix products, product(): jnp.dot(left, right, precision=largest_value, preferred_element_type=jnp....  67.4 us
    unnamed x1, blocking collectives  64.2 us
    another operation x10, other arithmetic, combine(): lower = jnp.linalg.cholesky(system)  47 us
    all_gather x1, blocking collectives, combine(): gain_rows = lax.all_gather(gain_pan, ('row', 'obs'), axis=0, tiled=True)  45.6 us
    all_gather x1, blocking collectives, per_device(): lax.all_gather(offsets, ('row', 'obs'), axis=1, tiled=True)  37.1 us
    another operation x8, other arithmetic, lower_solve(): return lax.linalg.triangular_solve(lower, rhs, left_side=True, lower=True)  30.5 us
    ppermute x5, starting transfers between devices, shifted(): return lax.ppermute(block, axis, route)  17.6 us
  transfers between devices with their start and end apart: 16, of which 6 were waited for; matrix products, arithmetic and copies ran while one was open for 33% of the time, Pallas kernels for 0%

profile of v1, /device:TPU:224, one launch (start us, length us, event | category | flops | bytes accessed | tf_op | source)
XLA Modules:
  0.0 530.4 jit_solution(13532728122809845748)
XLA Ops:
  8.8 13.0 %all_gather.37 = f32[2,128,256]{2,1,0:T(8,128)S(1)} all-gather(f32[2,32,256]{2,1,0:T(8,128)} %param.16), channel_id=1, replica_groups=mesh['tm'=8,'row'=8,'obs'=4] {'obs'}, dimensions={1}, use_global_device_ids=true | all-gather | bytes 327680 | tf_op jit(solution)/shard_map/all_gather | solution.py:100
  26.2 45.4 %all-reduce.7.cloned.1.call-done = f32[128,128]{1,0:T(8,128)} async-done(((f32[128,128]{1,0:T(8,128)}), f32[128,128]{1,0:T(8,128)}) %all-reduce.7.cloned.1.call-update) | async-done | bytes 65552 | tf_op jit(solution)/shard_map/psum | solution.py:73
  71.7 6.9 %all-gather.10.cloned.1.call-done = f32[2,1024,384]{2,1,0:T(8,128)} async-done(((f32[2,32,384]{2,1,0:T(8,128)}), f32[2,1024,384]{2,1,0:T(8,128)}) %all-gather.10.cloned.1.call-update) | async-done | bytes 3145744 | tf_op jit(solution)/shard_map/all_gather | solution.py:104
  81.8 3.6 reshape.312
  85.4 4.3 fusion.104
  91.7 4.9 convolution_bitcast_fusion.1
  98.3 41.5 %all-reduce.9.cloned.1.call-done = f32[128,128]{1,0:T(8,128)} async-done(((f32[128,128]{1,0:T(8,128)}), f32[128,128]{1,0:T(8,128)}) %all-reduce.9.cloned.1.call-update) | async-done | bytes 65552 | tf_op jit(solution)/shard_map/psum | solution.py:73
  141.5 11.7 %cholesky.60 = f32[128,128]{1,0:T(8,128)S(1)} custom-call(f32[128,128]{1,0:T(8,128)S(1)} %fusion.77), custom_call_target="Cholesky" | custom-call | tf_op jit(solution)/shard_map/jit(cholesky)/cholesky | solution.py:76
  154.6 9.8 %custom-call.31 = f32[1,128,128]{1,2,0:T(8,128)S(1)} custom-call(f32[1,128,128]{2,1,0:T(8,128)S(1)} %fusion.55), custom_call_target="InvertDiagBlocksLowerTriangular" | custom-call | tf_op jit(solution)/shard_map/triangular_solve/custom-call.4 | solution.py:21
  166.4 4.3 fusion.107
  176.4 3.3 collective-permute-start.1
  181.9 45.6 %all_gather.38 = f32[1024,128]{1,0:T(8,128)S(1)} all-gather(f32[32,128]{1,0:T(8,128)S(1)} %bitcast.273), channel_id=1, replica_groups=mesh['tm'=8,'row'=8,'obs'=4] {'row','obs'}, dimensions={0}, use_global_device_ids=true | all-gather | bytes 540672 | tf_op jit(solution)/shard_map/all_gather | solution.py:68
  227.5 5.4 %copy.79 = f32[128,8,8,128]{3,1,2,0:T(8,128)} copy(f32[128,8,8,128]{3,2,1,0:T(8,128)} %bitcast.259) | data formatting | bytes 8388608
  232.9 4.8 fusion.133
  238.8 4.8 fusion.52
  248.1 5.2 fusion.6
  253.3 4.5 collective-permute-start
  261.8 32.5 %all-reduce.11.cloned.1.call-done = f32[256,256]{0,1:T(8,128)} async-done(((f32[256,256]{0,1:T(8,128)}), f32[256,256]{0,1:T(8,128)}) %all-reduce.11.cloned.1.call-update) | async-done | bytes 262160 | tf_op jit(solution)/shard_map/psum | solution.py:73
  295.1 37.1 %all-gather = f32[32,32,2]{1,2,0:T(2,128)S(1)} all-gather(f32[1,32,2]{1,2,0:T(2,128)S(1)} %bitcast.282), channel_id=1, replica_groups=mesh['tm'=8,'row'=8,'obs'=4] {'row','obs'}, dimensions={0}, use_global_device_ids=true | all-gather | bytes 8448 | tf_op jit(solution)/shard_map/all_gather | solution.py:105
  332.3 7.9 %all-gather.1 = f32[4,32,2]{1,2,0:T(2,128)S(1)} all-gather(f32[1,32,2]{1,2,0:T(2,128)S(1)} %bitcast.288), channel_id=1, replica_groups=mesh['tm'=8,'row'=8,'obs'=4] {'obs'}, dimensions={0}, use_global_device_ids=true | all-gather | bytes 1280 | tf_op jit(solution)/shard_map/all_gather | solution.py:101
  341.5 6.7 %fusion.141 = f32[32,1024]{1,0:T(8,128)} fusion(f32[32,1024]{1,0:T(8,128)S(1)} %fusion.12, f32[1024,1024]{1,0:T(8,128)} %all-gather.12.cloned.1.call-done), kind=kOutput, calls=%fused_computation.205 | convolution fusion | flops 402653184 | bytes 4456448 | tf_op jit(solution)/shard_map/dot_general | solution.py:17
  354.4 3.3 collective-permute-start.3
  358.0 64.2 %all-reduce.1 = f32[1024]{0:T(1024)S(1)} all-reduce(f32[1024]{0:T(1024)S(1)} %dynamic-update-slice.17), channel_id=1, replica_groups=mesh['tm'=8,'row'=8,'obs'=4] {'row','obs'}, use_global_device_ids=true, to_apply=%add.1 | all-reduce | flops 1024 | bytes 8192
  426.2 5.8 %fusion.140 = f32[256,1024]{1,0:T(8,128)S(1)} fusion(f32[1024,256]{1,0:T(8,128)S(1)} %copy-done.4, f32[1024,1024]{1,0:T(8,128)} %all-gather.14.cloned.1.call-done), kind=kOutput, calls=%fused_computation.204 | convolution fusion | flops 3221225472 | bytes 6291456 | tf_op jit(solution)/shard_map/dot_general | solution.py:17
  434.1 11.7 %cholesky.115 = f32[128,128]{1,0:T(8,128)S(1)} custom-call(f32[128,128]{1,0:T(8,128)S(1)} %cholesky.141), custom_call_target="Cholesky" | custom-call | tf_op jit(solution)/shard_map/jit(cholesky)/cholesky | solution.py:76
  445.9 9.8 %custom-call.26 = f32[1,128,128]{1,2,0:T(8,128)S(1)} custom-call(f32[1,128,128]{2,1,0:T(8,128)S(1)} %get-tuple-element.62), custom_call_target="InvertDiagBlocksLowerTriangular" | custom-call | tf_op jit(solution)/shard_map/jit(cholesky)/cholesky | solution.py:76
  456.2 11.7 %cholesky.128 = f32[128,128]{1,0:T(8,128)S(1)} custom-call(f32[128,128]{1,0:T(8,128)S(1)} %convolution_subtract_fusion.3), custom_call_target="Cholesky" | custom-call | tf_op jit(solution)/shard_map/jit(cholesky)/cholesky | solution.py:76
  470.6 4.0 while.5
  474.6 19.9 %custom-call.33 = f32[2,128,128]{1,2,0:T(8,128)S(1)} custom-call(f32[2,128,128]{2,1,0:T(8,128)S(1)} %get-tuple-element.29), custom_call_target="InvertDiagBlocksLowerTriangular" | custom-call | tf_op jit(solution)/shard_map/triangular_solve/custom-call.5 | solution.py:21
  498.6 9.3 %fusion.139 = f32[256,1024]{1,0:T(8,128)S(1)} fusion(f32[1024,256]{1,0:T(8,128)} %all-gather.20.cloned.1.call-done, f32[1024,1024]{1,0:T(8,128)} %all-gather.12.cloned.1.call-done), kind=kOutput, calls=%fused_computation.203 | convolution fusion | flops 3221225472 | bytes 6291456 | tf_op jit(solution)/shard_map/dot_general | solution.py:17
  511.4 4.1 fusion.14
  517.3 5.4 %fusion.11 = f32[1,32,1024]{2,1,0:T(8,128)} fusion(f32[32,1024]{1,0:T(8,128)S(1)} %fusion.12, f32[32,1024]{1,0:T(8,128)S(1)} %collective-permute-done.4, f32[32,1024]{1,0:T(8,128)S(1)} %fusion.24, f32[1024,1024]{1,0:T(8,128)} %all-gather.22.cloned.1.call-done, f32[1024,1024]{1,0:T(8,128)} %all-gather.12.cloned.1.call-done, s32[]{:T(128)S(6)} %select_n.93, ...), kind=kOutput, calls=%fused_computation.20 | convolution fusion | flops 402751488 | bytes 4849669 | tf_op jit(solution)/shard_map/dot_general | solution.py:17
  (161 shorter events, 63.7 us)
Async XLA Ops:
  8.0 18.1 %copy-start.13 = (s32[2,8,3]{1,0,2:T(2,128)S(1)}, s32[2,8,3]{1,0,2:T(2,128)}, u32[]{:S(2)}) copy-start(s32[2,8,3]{1,0,2:T(2,128)} %param.11) | copy-start | bytes 580
  8.0 63.6 %all-reduce.7.cloned.1.call-start = ((), (), s32[]{:S(2)}) async-start(), calls=%async_computation.1 | async-start | bytes 131072 | tf_op jit(solution)/shard_map/psum | solution.py:73
  25.5 53.1 %all-gather.10.cloned.1.call-start = ((), (), s32[]{:S(2)}) async-start(), calls=%async_computation | async-start | bytes 3244032 | tf_op jit(solution)/shard_map/all_gather | solution.py:104
  26.1 113.6 %all-reduce.9.cloned.1.call-start = ((), (), s32[]{:S(2)}) async-start(), calls=%async_computation.2 | async-start | bytes 131072 | tf_op jit(solution)/shard_map/psum | solution.py:73
  71.6 167.2 %all-gather.18.cloned.1.call-start = ((), (), s32[]{:S(2)}) async-start(), calls=%async_computation.6 | async-start | bytes 4325376 | tf_op jit(solution)/shard_map/all_gather | solution.py:83
  81.8 9.9 %copy-start.8 = (f32[2,32,1024]{2,1,0:T(8,128)S(1)}, f32[2,32,1024]{2,1,0:T(8,128)}, u32[]{:S(2)}) copy-start(f32[2,32,1024]{2,1,0:T(8,128)} %param.14) | copy-start | bytes 786436
  89.7 2.0 copy-start
  96.7 147.4 %all-gather.16.cloned.1.call-start = ((), (), s32[]{:S(2)}) async-start(), calls=%async_computation.5 | async-start | bytes 1081344 | tf_op jit(solution)/shard_map/all_gather | solution.py:131
  98.2 72.4 %copy-start.7 = (f32[8,128,128]{2,1,0:T(8,128)}, f32[8,128,128]{2,1,0:T(8,128)S(1)}, u32[]{:S(2)}) copy-start(f32[8,128,128]{2,1,0:T(8,128)S(1)} %copy.56) | copy-start | bytes 1572868
  170.7 1.9 copy-start.2
  176.4 4.9 collective-permute-start.1
  181.2 0.6 copy-start.11
  181.9 112.4 %all-reduce.11.cloned.1.call-start = ((), (), s32[]{:S(2)}) async-start(), calls=%async_computation.7 | async-start | bytes 524288 | tf_op jit(solution)/shard_map/psum | solution.py:73
  227.5 5.4 %copy-start.1 = (f32[8,8,128,128]{3,1,2,0:T(8,128)S(1)}, f32[8,8,128,128]{3,1,2,0:T(8,128)}, u32[]{:S(2)}) copy-start(f32[8,8,128,128]{3,1,2,0:T(8,128)} %copy-done) | copy-start | bytes 12582916
  243.5 51.5 %copy-start.12 = (f32[2,32]{1,0:T(2,128)S(1)}, f32[2,32]{1,0:T(2,128)}, u32[]{:S(2)}) copy-start(f32[2,32]{1,0:T(2,128)} %param.13) | copy-start | bytes 772
  243.6 88.7 %copy-start.14 = (f32[2,32]{1,0:T(2,128)S(1)}, f32[2,32]{1,0:T(2,128)}, u32[]{:S(2)}) copy-start(f32[2,32]{1,0:T(2,128)} %param.17) | copy-start | bytes 772
  245.9 48.4 %copy-start.9 = (f32[32,256]{1,0:T(8,128)}, f32[32,256]{1,0:T(8,128)S(1)}, u32[]{:S(2)}) copy-start(f32[32,256]{1,0:T(8,128)S(1)} %fusion.138) | copy-start | bytes 98308
  247.8 100.5 %copy-start.15 = (u32[256]{0:T(256)S(1)}, u32[256]{0:T(256)}, u32[]{:S(2)}) copy-start(u32[256]{0:T(256)} %constant.217) | copy-start | bytes 3076
  247.8 93.7 %all-gather.12.cloned.1.call-start = ((), (), s32[]{:S(2)}) async-start(), calls=%async_computation.3 | async-start | bytes 4325376 | tf_op jit(solution)/shard_map/all_gather | solution.py:130
  253.3 7.7 %copy-start.5 = (f32[32,1024]{1,0:T(8,128)}, f32[32,1024]{1,0:T(8,128)S(1)}, u32[]{:S(2)}) copy-start(f32[32,1024]{1,0:T(8,128)S(1)} %fusion.6) | copy-start | bytes 393220
  253.3 168.9 %copy-start.4 = (f32[1024,256]{1,0:T(8,128)S(1)}, f32[1024,256]{1,0:T(8,128)}, u32[]{:S(2)}) copy-start(f32[1024,256]{1,0:T(8,128)} %all-gather.16.cloned.1.call-done) | copy-start | bytes 3145732
  253.3 7.0 %collective-permute-start = (f32[32,1024]{1,0:T(8,128)S(1)}, f32[32,1024]{1,0:T(8,128)S(1)}, u32[]{:S(2)}, u32[]{:S(2)}) collective-permute-start(f32[32,1024]{1,0:T(8,128)S(1)} %fusion.6), channel_id=1, source_target_pairs={{32,0},{64,32},{96,64},{128,96},{160,128},{192,160},{224,192},{33,... | collective-permute-start | bytes 393224 | tf_op jit(solution)/shard_map/ppermute | solution.py:13
  260.3 0.7 copy-start.10
  261.0 165.2 %all-gather.14.cloned.1.call-start = ((), (), s32[]{:S(2)}) async-start(), calls=%async_computation.4 | async-start | bytes 4325376 | tf_op jit(solution)/shard_map/all_gather | solution.py:129
  261.7 170.3 %all-reduce.13.cloned.1.call-start = ((), (), s32[]{:S(2)}) async-start(), calls=%async_computation.8 | async-start | bytes 524288 | tf_op jit(solution)/shard_map/psum | solution.py:73
  294.3 204.4 %all-gather.20.cloned.1.call-start = ((), (), s32[]{:S(2)}) async-start(), calls=%async_computation.9 | async-start | bytes 1081344 | tf_op jit(solution)/shard_map/all_gather | solution.py:68
  295.0 222.3 %all-gather.22.cloned.1.call-start = ((), (), s32[]{:S(2)}) async-start(), calls=%async_computation.10 | async-start | bytes 4325376 | tf_op jit(solution)/shard_map/all_gather | solution.py:83
  349.7 73.1 %collective-permute-start.2 = (f32[256]{0:T(256)S(1)}, f32[256]{0:T(256)S(1)}, u32[]{:S(2)}, u32[]{:S(2)}) collective-permute-start(f32[256]{0:T(256)S(1)} %pad_maximum_fusion.5), channel_id=1, source_target_pairs={{32,0},{64,32},{96,64},{128,96},{160,128},{192,160},{224,192},{33,... | collective-permute-start | bytes 3080 | tf_op jit(solution)/shard_map/ppermute | solution.py:13
  354.4 161.3 %collective-permute-start.3 = (f32[32]{0:T(128)S(1)}, f32[32]{0:T(128)S(1)}, u32[]{:S(2)}, u32[]{:S(2)}) collective-permute-start(f32[32]{0:T(128)S(1)} %fusion.16), channel_id=1, source_target_pairs={{32,0},{64,32},{96,64},{128,96},{160,128},{192,160},{224,192},{33,... | collective-permute-start | bytes 392 | tf_op jit(solution)/shard_map/ppermute | solution.py:13
  422.8 94.5 %collective-permute-start.4 = (f32[32,1024]{1,0:T(8,128)S(1)}, f32[32,1024]{1,0:T(8,128)S(1)}, u32[]{:S(2)}, u32[]{:S(2)}) collective-permute-start(f32[32,1024]{1,0:T(8,128)S(1)} %fusion.12), channel_id=1, source_target_pairs={{32,0},{64,32},{96,64},{128,96},{160,128},{192,160},{224,192},{33,... | collective-permute-start | bytes 393224 | tf_op jit(solution)/shard_map/ppermute | solution.py:13
  507.9 3.5 copy-start.3
  507.9 3.5 copy-start.6
Sparse Core Ops, SparseCore 0:
  25.6 45.9 all-reduce.6
  74.0 65.6 all-reduce.8
  247.9 46.2 all-reduce.10
  296.5 66.9 all-reduce.12
Sparse Core Ops, SparseCore 1:
  28.6 50.0 all-gather.9
  96.7 50.6 all-gather.17
  182.0 48.5 all-gather.15
  261.0 49.6 all-gather.11
  313.8 50.9 all-gather.13
  367.4 47.3 all-gather.19
  417.2 50.9 all-gather.21
